TPU v7x, 128 devices: a whole 4x4x4 slice. The times are simulated.
128 devices in a mesh: grid: 16 (over z_lo, y, core), sta: 8 (over z_hi, x).
Axes of the slice: x: 4, y: 4, z: 4 (z_hi: 2, z_lo: 2; z = z_hi * 2 + z_lo), core: 2. Of those that a mesh axis runs over, the one named last changes fastest.
Arguments:
- spectra: bfloat16 [64, 2, 6144], P(None, None, 'sta'), may hold values from -6 to 6
- lag_samples: int32 [16, 6144], P('grid', 'sta'), may hold values from 0 to 5999
- slowness: bfloat16 [16, 3, 6144], P('grid', None, 'sta'), may hold values from -3 to 3
- spread_taps: float32 [3, 17], replicated, may hold values from 0.02 to 0.2
Outputs:
- stacked: float32 [16, 32, 8, 128], P('grid')
- deblurred: float32 [16, 32, 8, 128], P('grid')
All inputs are finite; a program needn't handle non-finite values.
Results may differ from a plain program's by a relative error of at most 0.0015.
Values may be sent and summed in bfloat16 or wider, within the bound.
A program may use at most 64 MiB of HBM per device.

v0:
```python
import math
import jax
import jax.numpy as jnp
from jax import lax
from jax.sharding import PartitionSpec as P

STATIONS = 6144
FREQS = 64
F0 = 600
NT = 6000
TAPS = 17
HALF = 8
ITERS = 4
CX = 32
CY = 8
CZ = 128
TWO_PI = 2.0 * math.pi
BACKGROUND = 0.05


def with_halo(array, sides, width):
    for axis, dim in sides:
        size, length = (lax.axis_size(axis), array.shape[dim])
        up = [(i, (i + 1) % size) for i in range(size - 1)]
        down = [(j, i) for i, j in up]
        last = lax.slice_in_dim(array, length - width, length, axis=dim)
        leading = lax.slice_in_dim(array, 0, width, axis=dim)
        before = lax.ppermute(last, axis, up)
        after = lax.ppermute(leading, axis, down)
        array = jnp.concatenate([before, array, after], axis=dim)
    return array


def align_rows(spectra, lag_row):
    bins = F0 + jnp.arange(FREQS, dtype=jnp.int32)
    cycles = bins[:, None] * lag_row[None, :] % NT
    turned = cycles.astype(jnp.float32) * (TWO_PI / NT)
    cosine = jnp.cos(turned)
    sine = jnp.sin(turned)
    real_in = spectra[:, 0, :].astype(jnp.float32)
    imag_in = spectra[:, 1, :].astype(jnp.float32)
    real_out = real_in * cosine + imag_in * sine
    imag_out = imag_in * cosine - real_in * sine
    return jnp.stack([real_out, imag_out], axis=1).astype(jnp.bfloat16)


def beam_freq(freq, aligned_row, slow_rows):
    omega = (F0 + freq).astype(jnp.float32) * (TWO_PI / NT)
    slow = slow_rows.astype(jnp.float32)
    x_coord = jnp.arange(CX, dtype=jnp.float32) - (CX - 1) / 2.0
    y_coord = jnp.arange(CY, dtype=jnp.float32) - (CY - 1) / 2.0
    z_coord = jnp.arange(CZ, dtype=jnp.float32) - (CZ - 1) / 2.0
    phase_x = (omega * slow[0])[None, :] * x_coord[:, None]
    phase_y = (omega * slow[1])[None, :] * y_coord[:, None]
    phase = phase_x[:, None, :] + phase_y[None, :, :]
    cosine = jnp.cos(phase)
    sine = jnp.sin(phase)
    real_in = aligned_row[0].astype(jnp.float32)[None, None, :]
    imag_in = aligned_row[1].astype(jnp.float32)[None, None, :]
    front_real = (real_in * cosine + imag_in * sine).astype(jnp.bfloat16).reshape(CX * CY, -1)
    front_imag = (imag_in * cosine - real_in * sine).astype(jnp.bfloat16).reshape(CX * CY, -1)
    left_side = jnp.concatenate([front_real, front_imag], axis=1)
    phase_z = (omega * slow[2])[:, None] * z_coord[None, :]
    depth_real = jnp.cos(phase_z).astype(jnp.bfloat16)
    depth_imag = jnp.sin(phase_z).astype(jnp.bfloat16)
    upper_rows = jnp.concatenate([depth_real, -depth_imag], axis=1)
    lower_rows = jnp.concatenate([depth_imag, depth_real], axis=1)
    right_side = jnp.concatenate([upper_rows, lower_rows], axis=0)
    return jnp.dot(left_side, right_side, preferred_element_type=jnp.float32)


def freq_beams(freq_ids, aligned_rows, slow_rows):
    return lax.map(lambda pair: beam_freq(pair[0], pair[1], slow_rows), (freq_ids, aligned_rows))


def band_matrix(taps, length):
    rows = jnp.arange(length, dtype=jnp.int32)[:, None]
    columns = jnp.arange(length + 2 * HALF, dtype=jnp.int32)[None, :]
    offset = columns - rows
    picks = jnp.arange(TAPS, dtype=jnp.int32)[:, None, None]
    return jnp.sum(jnp.where(offset[None] == picks, taps[:, None, None], 0.0), axis=0)


def blur(volume, bands):
    band_x, square_y, square_z = bands
    padded = with_halo(volume.astype(jnp.bfloat16), (("grid", 0),), HALF).astype(volume.dtype)
    along_x = jnp.einsum("ip,pyz->iyz", band_x, padded, precision=lax.Precision.HIGHEST)
    along_y = jnp.einsum("jq,xqz->xjz", square_y, along_x, precision=lax.Precision.HIGHEST)
    return jnp.einsum("xyw,kw->xyk", along_y, square_z, precision=lax.Precision.HIGHEST)


def per_device(spectra, lag_samples, slowness, spread_taps):
    groups = lax.axis_size("sta")
    own_count = FREQS // groups
    first_bin = lax.axis_index("sta") * own_count
    aligned = align_rows(spectra, lag_samples[0])
    own_ids = first_bin + jnp.arange(own_count, dtype=jnp.int32)
    rows = lax.dynamic_slice_in_dim(
        lax.all_gather(aligned, "sta", axis=2, tiled=True), first_bin, own_count, 0
    )
    beams = freq_beams(own_ids, rows, lax.all_gather(slowness, "sta", axis=2, tiled=True)[0])
    squares = jnp.sum(beams * beams, axis=0)
    local_power = squares[:, :CZ] + squares[:, CZ:]
    summed = lax.psum(local_power, "sta")
    stacked = (summed / (FREQS * STATIONS) + BACKGROUND).reshape(CX, CY, CZ)
    square_y = band_matrix(spread_taps[1], CY)[:, HALF : HALF + CY]
    square_z = band_matrix(spread_taps[2], CZ)[:, HALF : HALF + CZ]
    bands = (band_matrix(spread_taps[0], CX), square_y, square_z)
    estimate = stacked
    for sweep in range(ITERS):
        blurred = blur(estimate, bands)
        estimate = estimate * blur(stacked / blurred, bands)
    return (stacked[None], estimate[None])


def solution(mesh):
    placed = (P(None, None, "sta"), P("grid", "sta"), P("grid", None, "sta"), P())
    return jax.shard_map(
        per_device,
        mesh=mesh,
        in_specs=placed,
        out_specs=(P("grid", None, None, None), P("grid", None, None, None)),
        check_vma=False,
    )
```

profile of v0, /device:TPU:25, one launch (start us, length us, event | category | flops | bytes accessed | tf_op | source)
XLA Modules:
  0.0 648.4 jit_solution(14156776172203744260)
XLA Ops:
  11.0 29.4 %all_gather.7 = bf16[1,3,6144]{2,1,0:T(4,128)(2,1)S(1)} all-gather(bf16[1,3,768]{2,1,0:T(4,128)(2,1)} %param.8), channel_id=1, replica_groups=mesh['grid'=16,'sta'=8] {'sta'}, dimensions={2}, use_global_device_ids=true | all-gather | bytes 41472 | tf_op jit(solution)/shard_map/all_gather | solution.py:101
  41.5 21.8 %all-gather.2.cloned.1.call-done = bf16[64,2,6144]{2,0,1:T(8,128)(2,1)} async-done(((bf16[64,2,768]{2,0,1:T(8,128)(2,1)}), bf16[64,2,6144]{2,0,1:T(8,128)(2,1)}) %all-gather.2.cloned.1.call-update) | async-done | bytes 1572880 | tf_op jit(solution)/shard_map/all_gather | solution.py:99
  64.4 408.7 %while.12 = (s32[]{:T(128)}, f32[8,256,256]{2,1,0:T(8,128)S(1)}, bf16[8,2,6144]{2,1,0:T(2,128)(2,1)S(1)}, s32[8]{0:T(128)S(1)}, bf16[3,6144]{1,0:T(4,128)(2,1)S(...) while((s32[]{:T(128)}, f32[8,256,256]{2,1,0:T(8,128)S(1)}, ...), condition=%wide.region_1.2_spmd, body=%wide.region_0.1_spmd.sunk | while | flops 1669103744 | bytes 24729580 | solution.py:73
  66.0 23.7 %fusion.136 = (bf16[256,6144]{1,0:T(8,128)(2,1)S(1)}, bf16[256,6144]{1,0:T(8,128)(2,1)S(1)}) fusion(f32[6144]{0:T(1024)S(1)} %bitcast.160, f32[8,6144]{1,0:T(8,128)S(1)} %broadcast_multiply_fusion.4, f32[32,6144]{1,0:T(8,128)S(1)} %broadcast_multiply_fusion.5, f32[6144]{0:T(1024)S(1)} %bitcast.159), kind=kLoop, calls=%fused_computation.6.clone.1 | loop fusion | flops 14155776 | bytes 7323648 | tf_op jit(solution)/shard_map/while/body/eval_jaxpr/convert_element_type | solution.py:60
  89.8 12.3 %fusion.134 = (bf16[6144,128]{1,0:T(8,128)(2,1)S(1)}, bf16[6144,128]{1,0:T(8,128)(2,1)S(1)}) fusion(f32[128]{0:T(128)S(1)} %iota_add_fusion.8, f32[6144]{0:T(1024)S(1)} %bitcast.157), kind=kLoop, calls=%fused_computation.26.clone.2 | loop fusion | flops 2359296 | bytes 3170816 | tf_op jit(solution)/shard_map/while/body/eval_jaxpr/convert_element_type | solution.py:65
  102.1 11.5 %fusion.135 = bf16[6144,128]{1,0:T(8,128)(2,1)S(1)} fusion(f32[128]{0:T(128)S(1)} %iota_add_fusion.8, f32[6144]{0:T(1024)S(1)} %bitcast.158), kind=kLoop, calls=%fused_computation.30.clone.1 | loop fusion | flops 3932160 | bytes 1597952 | tf_op jit(solution)/shard_map/while/body/eval_jaxpr/neg | solution.py:66
  117.1 23.7 %fusion.136 = (bf16[256,6144]{1,0:T(8,128)(2,1)S(1)}, bf16[256,6144]{1,0:T(8,128)(2,1)S(1)}) fusion(f32[6144]{0:T(1024)S(1)} %bitcast.160, f32[8,6144]{1,0:T(8,128)S(1)} %broadcast_multiply_fusion.4, f32[32,6144]{1,0:T(8,128)S(1)} %broadcast_multiply_fusion.5, f32[6144]{0:T(1024)S(1)} %bitcast.159), kind=kLoop, calls=%fused_computation.6.clone.1 | loop fusion | flops 14155776 | bytes 7323648 | tf_op jit(solution)/shard_map/while/body/eval_jaxpr/convert_element_type | solution.py:60
  140.9 12.3 %fusion.134 = (bf16[6144,128]{1,0:T(8,128)(2,1)S(1)}, bf16[6144,128]{1,0:T(8,128)(2,1)S(1)}) fusion(f32[128]{0:T(128)S(1)} %iota_add_fusion.8, f32[6144]{0:T(1024)S(1)} %bitcast.157), kind=kLoop, calls=%fused_computation.26.clone.2 | loop fusion | flops 2359296 | bytes 3170816 | tf_op jit(solution)/shard_map/while/body/eval_jaxpr/convert_element_type | solution.py:65
  153.2 11.5 %fusion.135 = bf16[6144,128]{1,0:T(8,128)(2,1)S(1)} fusion(f32[128]{0:T(128)S(1)} %iota_add_fusion.8, f32[6144]{0:T(1024)S(1)} %bitcast.158), kind=kLoop, calls=%fused_computation.30.clone.1 | loop fusion | flops 3932160 | bytes 1597952 | tf_op jit(solution)/shard_map/while/body/eval_jaxpr/neg | solution.py:66
  168.2 23.7 %fusion.136 = (bf16[256,6144]{1,0:T(8,128)(2,1)S(1)}, bf16[256,6144]{1,0:T(8,128)(2,1)S(1)}) fusion(f32[6144]{0:T(1024)S(1)} %bitcast.160, f32[8,6144]{1,0:T(8,128)S(1)} %broadcast_multiply_fusion.4, f32[32,6144]{1,0:T(8,128)S(1)} %broadcast_multiply_fusion.5, f32[6144]{0:T(1024)S(1)} %bitcast.159), kind=kLoop, calls=%fused_computation.6.clone.1 | loop fusion | flops 14155776 | bytes 7323648 | tf_op jit(solution)/shard_map/while/body/eval_jaxpr/convert_element_type | solution.py:60
  192.0 12.3 %fusion.134 = (bf16[6144,128]{1,0:T(8,128)(2,1)S(1)}, bf16[6144,128]{1,0:T(8,128)(2,1)S(1)}) fusion(f32[128]{0:T(128)S(1)} %iota_add_fusion.8, f32[6144]{0:T(1024)S(1)} %bitcast.157), kind=kLoop, calls=%fused_computation.26.clone.2 | loop fusion | flops 2359296 | bytes 3170816 | tf_op jit(solution)/shard_map/while/body/eval_jaxpr/convert_element_type | solution.py:65
  204.3 11.5 %fusion.135 = bf16[6144,128]{1,0:T(8,128)(2,1)S(1)} fusion(f32[128]{0:T(128)S(1)} %iota_add_fusion.8, f32[6144]{0:T(1024)S(1)} %bitcast.158), kind=kLoop, calls=%fused_computation.30.clone.1 | loop fusion | flops 3932160 | bytes 1597952 | tf_op jit(solution)/shard_map/while/body/eval_jaxpr/neg | solution.py:66
  219.3 23.7 %fusion.136 = (bf16[256,6144]{1,0:T(8,128)(2,1)S(1)}, bf16[256,6144]{1,0:T(8,128)(2,1)S(1)}) fusion(f32[6144]{0:T(1024)S(1)} %bitcast.160, f32[8,6144]{1,0:T(8,128)S(1)} %broadcast_multiply_fusion.4, f32[32,6144]{1,0:T(8,128)S(1)} %broadcast_multiply_fusion.5, f32[6144]{0:T(1024)S(1)} %bitcast.159), kind=kLoop, calls=%fused_computation.6.clone.1 | loop fusion | flops 14155776 | bytes 7323648 | tf_op jit(solution)/shard_map/while/body/eval_jaxpr/convert_element_type | solution.py:60
  243.0 12.3 %fusion.134 = (bf16[6144,128]{1,0:T(8,128)(2,1)S(1)}, bf16[6144,128]{1,0:T(8,128)(2,1)S(1)}) fusion(f32[128]{0:T(128)S(1)} %iota_add_fusion.8, f32[6144]{0:T(1024)S(1)} %bitcast.157), kind=kLoop, calls=%fused_computation.26.clone.2 | loop fusion | flops 2359296 | bytes 3170816 | tf_op jit(solution)/shard_map/while/body/eval_jaxpr/convert_element_type | solution.py:65
  255.4 11.5 %fusion.135 = bf16[6144,128]{1,0:T(8,128)(2,1)S(1)} fusion(f32[128]{0:T(128)S(1)} %iota_add_fusion.8, f32[6144]{0:T(1024)S(1)} %bitcast.158), kind=kLoop, calls=%fused_computation.30.clone.1 | loop fusion | flops 3932160 | bytes 1597952 | tf_op jit(solution)/shard_map/while/body/eval_jaxpr/neg | solution.py:66
  270.4 23.7 %fusion.136 = (bf16[256,6144]{1,0:T(8,128)(2,1)S(1)}, bf16[256,6144]{1,0:T(8,128)(2,1)S(1)}) fusion(f32[6144]{0:T(1024)S(1)} %bitcast.160, f32[8,6144]{1,0:T(8,128)S(1)} %broadcast_multiply_fusion.4, f32[32,6144]{1,0:T(8,128)S(1)} %broadcast_multiply_fusion.5, f32[6144]{0:T(1024)S(1)} %bitcast.159), kind=kLoop, calls=%fused_computation.6.clone.1 | loop fusion | flops 14155776 | bytes 7323648 | tf_op jit(solution)/shard_map/while/body/eval_jaxpr/convert_element_type | solution.py:60
  294.1 12.3 %fusion.134 = (bf16[6144,128]{1,0:T(8,128)(2,1)S(1)}, bf16[6144,128]{1,0:T(8,128)(2,1)S(1)}) fusion(f32[128]{0:T(128)S(1)} %iota_add_fusion.8, f32[6144]{0:T(1024)S(1)} %bitcast.157), kind=kLoop, calls=%fused_computation.26.clone.2 | loop fusion | flops 2359296 | bytes 3170816 | tf_op jit(solution)/shard_map/while/body/eval_jaxpr/convert_element_type | solution.py:65
  306.5 11.5 %fusion.135 = bf16[6144,128]{1,0:T(8,128)(2,1)S(1)} fusion(f32[128]{0:T(128)S(1)} %iota_add_fusion.8, f32[6144]{0:T(1024)S(1)} %bitcast.158), kind=kLoop, calls=%fused_computation.30.clone.1 | loop fusion | flops 3932160 | bytes 1597952 | tf_op jit(solution)/shard_map/while/body/eval_jaxpr/neg | solution.py:66
  321.5 23.7 %fusion.136 = (bf16[256,6144]{1,0:T(8,128)(2,1)S(1)}, bf16[256,6144]{1,0:T(8,128)(2,1)S(1)}) fusion(f32[6144]{0:T(1024)S(1)} %bitcast.160, f32[8,6144]{1,0:T(8,128)S(1)} %broadcast_multiply_fusion.4, f32[32,6144]{1,0:T(8,128)S(1)} %broadcast_multiply_fusion.5, f32[6144]{0:T(1024)S(1)} %bitcast.159), kind=kLoop, calls=%fused_computation.6.clone.1 | loop fusion | flops 14155776 | bytes 7323648 | tf_op jit(solution)/shard_map/while/body/eval_jaxpr/convert_element_type | solution.py:60
  345.2 12.3 %fusion.134 = (bf16[6144,128]{1,0:T(8,128)(2,1)S(1)}, bf16[6144,128]{1,0:T(8,128)(2,1)S(1)}) fusion(f32[128]{0:T(128)S(1)} %iota_add_fusion.8, f32[6144]{0:T(1024)S(1)} %bitcast.157), kind=kLoop, calls=%fused_computation.26.clone.2 | loop fusion | flops 2359296 | bytes 3170816 | tf_op jit(solution)/shard_map/while/body/eval_jaxpr/convert_element_type | solution.py:65
  357.6 11.5 %fusion.135 = bf16[6144,128]{1,0:T(8,128)(2,1)S(1)} fusion(f32[128]{0:T(128)S(1)} %iota_add_fusion.8, f32[6144]{0:T(1024)S(1)} %bitcast.158), kind=kLoop, calls=%fused_computation.30.clone.1 | loop fusion | flops 3932160 | bytes 1597952 | tf_op jit(solution)/shard_map/while/body/eval_jaxpr/neg | solution.py:66
  372.5 23.7 %fusion.136 = (bf16[256,6144]{1,0:T(8,128)(2,1)S(1)}, bf16[256,6144]{1,0:T(8,128)(2,1)S(1)}) fusion(f32[6144]{0:T(1024)S(1)} %bitcast.160, f32[8,6144]{1,0:T(8,128)S(1)} %broadcast_multiply_fusion.4, f32[32,6144]{1,0:T(8,128)S(1)} %broadcast_multiply_fusion.5, f32[6144]{0:T(1024)S(1)} %bitcast.159), kind=kLoop, calls=%fused_computation.6.clone.1 | loop fusion | flops 14155776 | bytes 7323648 | tf_op jit(solution)/shard_map/while/body/eval_jaxpr/convert_element_type | solution.py:60
  396.3 12.3 %fusion.134 = (bf16[6144,128]{1,0:T(8,128)(2,1)S(1)}, bf16[6144,128]{1,0:T(8,128)(2,1)S(1)}) fusion(f32[128]{0:T(128)S(1)} %iota_add_fusion.8, f32[6144]{0:T(1024)S(1)} %bitcast.157), kind=kLoop, calls=%fused_computation.26.clone.2 | loop fusion | flops 2359296 | bytes 3170816 | tf_op jit(solution)/shard_map/while/body/eval_jaxpr/convert_element_type | solution.py:65
  408.6 11.5 %fusion.135 = bf16[6144,128]{1,0:T(8,128)(2,1)S(1)} fusion(f32[128]{0:T(128)S(1)} %iota_add_fusion.8, f32[6144]{0:T(1024)S(1)} %bitcast.158), kind=kLoop, calls=%fused_computation.30.clone.1 | loop fusion | flops 3932160 | bytes 1597952 | tf_op jit(solution)/shard_map/while/body/eval_jaxpr/neg | solution.py:66
  423.6 23.7 %fusion.136 = (bf16[256,6144]{1,0:T(8,128)(2,1)S(1)}, bf16[256,6144]{1,0:T(8,128)(2,1)S(1)}) fusion(f32[6144]{0:T(1024)S(1)} %bitcast.160, f32[8,6144]{1,0:T(8,128)S(1)} %broadcast_multiply_fusion.4, f32[32,6144]{1,0:T(8,128)S(1)} %broadcast_multiply_fusion.5, f32[6144]{0:T(1024)S(1)} %bitcast.159), kind=kLoop, calls=%fused_computation.6.clone.1 | loop fusion | flops 14155776 | bytes 7323648 | tf_op jit(solution)/shard_map/while/body/eval_jaxpr/convert_element_type | solution.py:60
  447.4 12.3 %fusion.134 = (bf16[6144,128]{1,0:T(8,128)(2,1)S(1)}, bf16[6144,128]{1,0:T(8,128)(2,1)S(1)}) fusion(f32[128]{0:T(128)S(1)} %iota_add_fusion.8, f32[6144]{0:T(1024)S(1)} %bitcast.157), kind=kLoop, calls=%fused_computation.26.clone.2 | loop fusion | flops 2359296 | bytes 3170816 | tf_op jit(solution)/shard_map/while/body/eval_jaxpr/convert_element_type | solution.py:65
  459.7 11.5 %fusion.135 = bf16[6144,128]{1,0:T(8,128)(2,1)S(1)} fusion(f32[128]{0:T(128)S(1)} %iota_add_fusion.8, f32[6144]{0:T(1024)S(1)} %bitcast.158), kind=kLoop, calls=%fused_computation.30.clone.1 | loop fusion | flops 3932160 | bytes 1597952 | tf_op jit(solution)/shard_map/while/body/eval_jaxpr/neg | solution.py:66
  474.1 78.1 %all-reduce.2.cloned.1.call-done = f32[256,128]{1,0:T(8,128)} async-done(((f32[256,128]{1,0:T(8,128)}), f32[256,128]{1,0:T(8,128)}) %all-reduce.2.cloned.1.call-update) | async-done | bytes 131088 | tf_op jit(solution)/shard_map/psum | solution.py:104
  553.2 8.2 %collective-permute-start = (bf16[8,8,128]{2,0,1:T(8,128)(2,1)S(1)}, bf16[8,8,128]{2,0,1:T(8,128)(2,1)S(1)}, u32[]{:S(2)}, u32[]{:S(2)}) collective-permute-start(bf16[8,8,128]{2,0,1:T(8,128)(2,1)S(1)} %get-tuple-element.119), channel_id=1, source_target_pairs={{0,8},{8,16},{16,24},{24,32},{32,40},{40,48},{48,56},{56,64},{64,7... | collective-permute-start | bytes 49160 | tf_op jit(solution)/shard_map/ppermute | solution.py:28
  563.5 5.1 collective-permute-done.1
  595.5 4.8 collective-permute-done.7
  625.4 4.8 collective-permute-done.13
  (174 shorter events, 94.9 us)
Async XLA Ops:
  7.2 56.1 %all-gather.2.cloned.1.call-start = ((), (), s32[]{:S(2)}) async-start(), calls=%async_computation | async-start | bytes 1769472 | tf_op jit(solution)/shard_map/all_gather | solution.py:99
  11.0 541.2 %all-reduce.2.cloned.1.call-start = ((), (), s32[]{:S(2)}) async-start(), calls=%async_computation.1 | async-start | bytes 262144 | tf_op jit(solution)/shard_map/psum | solution.py:104
  552.2 38.7 %copy-start = (f32[256,128]{1,0:T(8,128)S(1)}, f32[256,128]{1,0:T(8,128)}, u32[]{:S(2)}) copy-start(f32[256,128]{1,0:T(8,128)} %all-reduce.2.cloned.1.call-done) | copy-start | bytes 393220
  553.2 10.3 %collective-permute-start = (bf16[8,8,128]{2,0,1:T(8,128)(2,1)S(1)}, bf16[8,8,128]{2,0,1:T(8,128)(2,1)S(1)}, u32[]{:S(2)}, u32[]{:S(2)}) collective-permute-start(bf16[8,8,128]{2,0,1:T(8,128)(2,1)S(1)} %get-tuple-element.119), channel_id=1, source_target_pairs={{0,8},{8,16},{16,24},{24,32},{32,40},{40,48},{48,56},{56,64},{64,7... | collective-permute-start | bytes 49160 | tf_op jit(solution)/shard_map/ppermute | solution.py:28
  561.5 7.2 %collective-permute-start.1 = (bf16[8,8,128]{2,0,1:T(8,128)(2,1)S(1)}, bf16[8,8,128]{2,0,1:T(8,128)(2,1)S(1)}, u32[]{:S(2)}, u32[]{:S(2)}) collective-permute-start(bf16[8,8,128]{2,0,1:T(8,128)(2,1)S(1)} %get-tuple-element.120), channel_id=1, source_target_pairs={{8,0},{16,8},{24,16},{32,24},{40,32},{48,40},{56,48},{64,56},{72,6... | collective-permute-start | bytes 49160 | tf_op jit(solution)/shard_map/ppermute | solution.py:29
  570.4 4.3 collective-permute-start.2
  572.3 7.2 %collective-permute-start.3 = (bf16[8,8,128]{2,1,0:T(8,128)(2,1)S(1)}, bf16[8,8,128]{2,1,0:T(8,128)(2,1)S(1)}, u32[]{:S(2)}, u32[]{:S(2)}) collective-permute-start(bf16[8,8,128]{2,1,0:T(8,128)(2,1)S(1)} %get-tuple-element.118), channel_id=1, source_target_pairs={{8,0},{16,8},{24,16},{32,24},{40,32},{48,40},{56,48},{64,56},{72,6... | collective-permute-start | bytes 49160 | tf_op jit(solution)/shard_map/ppermute | solution.py:29
  581.2 4.3 collective-permute-start.4
  583.1 7.2 %collective-permute-start.5 = (bf16[8,8,128]{2,1,0:T(8,128)(2,1)S(1)}, bf16[8,8,128]{2,1,0:T(8,128)(2,1)S(1)}, u32[]{:S(2)}, u32[]{:S(2)}) collective-permute-start(bf16[8,8,128]{2,1,0:T(8,128)(2,1)S(1)} %get-tuple-element.116), channel_id=1, source_target_pairs={{8,0},{16,8},{24,16},{32,24},{40,32},{48,40},{56,48},{64,56},{72,6... | collective-permute-start | bytes 49160 | tf_op jit(solution)/shard_map/ppermute | solution.py:29
  591.2 4.3 collective-permute-start.6
  593.1 7.2 %collective-permute-start.7 = (bf16[8,8,128]{2,1,0:T(8,128)(2,1)S(1)}, bf16[8,8,128]{2,1,0:T(8,128)(2,1)S(1)}, u32[]{:S(2)}, u32[]{:S(2)}) collective-permute-start(bf16[8,8,128]{2,1,0:T(8,128)(2,1)S(1)} %get-tuple-element.114), channel_id=1, source_target_pairs={{8,0},{16,8},{24,16},{32,24},{40,32},{48,40},{56,48},{64,56},{72,6... | collective-permute-start | bytes 49160 | tf_op jit(solution)/shard_map/ppermute | solution.py:29
  601.1 4.5 collective-permute-start.8
  603.1 7.2 %collective-permute-start.9 = (bf16[8,8,128]{2,1,0:T(8,128)(2,1)S(1)}, bf16[8,8,128]{2,1,0:T(8,128)(2,1)S(1)}, u32[]{:S(2)}, u32[]{:S(2)}) collective-permute-start(bf16[8,8,128]{2,1,0:T(8,128)(2,1)S(1)} %get-tuple-element.112), channel_id=1, source_target_pairs={{8,0},{16,8},{24,16},{32,24},{40,32},{48,40},{56,48},{64,56},{72,6... | collective-permute-start | bytes 49160 | tf_op jit(solution)/shard_map/ppermute | solution.py:29
  611.1 4.3 collective-permute-start.10
  613.0 7.2 %collective-permute-start.11 = (bf16[8,8,128]{2,1,0:T(8,128)(2,1)S(1)}, bf16[8,8,128]{2,1,0:T(8,128)(2,1)S(1)}, u32[]{:S(2)}, u32[]{:S(2)}) collective-permute-start(bf16[8,8,128]{2,1,0:T(8,128)(2,1)S(1)} %get-tuple-element.110), channel_id=1, source_target_pairs={{8,0},{16,8},{24,16},{32,24},{40,32},{48,40},{56,48},{64,56},{72,6... | collective-permute-start | bytes 49160 | tf_op jit(solution)/shard_map/ppermute | solution.py:29
  621.0 4.3 collective-permute-start.12
  623.0 7.2 %collective-permute-start.13 = (bf16[8,8,128]{2,1,0:T(8,128)(2,1)S(1)}, bf16[8,8,128]{2,1,0:T(8,128)(2,1)S(1)}, u32[]{:S(2)}, u32[]{:S(2)}) collective-permute-start(bf16[8,8,128]{2,1,0:T(8,128)(2,1)S(1)} %get-tuple-element.108), channel_id=1, source_target_pairs={{8,0},{16,8},{24,16},{32,24},{40,32},{48,40},{56,48},{64,56},{72,6... | collective-permute-start | bytes 49160 | tf_op jit(solution)/shard_map/ppermute | solution.py:29
  631.0 5.0 collective-permute-start.14
  632.9 7.2 %collective-permute-start.15 = (bf16[8,8,128]{2,1,0:T(8,128)(2,1)S(1)}, bf16[8,8,128]{2,1,0:T(8,128)(2,1)S(1)}, u32[]{:S(2)}, u32[]{:S(2)}) collective-permute-start(bf16[8,8,128]{2,1,0:T(8,128)(2,1)S(1)} %get-tuple-element.106), channel_id=1, source_target_pairs={{8,0},{16,8},{24,16},{32,24},{40,32},{48,40},{56,48},{64,56},{72,6... | collective-permute-start | bytes 49160 | tf_op jit(solution)/shard_map/ppermute | solution.py:29
Sparse Core Ops, SparseCore 0:
  11.1 52.1 all-gather.1
  474.1 78.0 all-reduce.1
where the time goes:
time: 649 us; the launch traced here: 648 us
  other arithmetic  389 us (60%)
  waiting for transfers between devices  138 us (21%)
  starting transfers between devices  40.7 us (6%)
  blocking collectives  29.4 us (5%)
  matrix products  23.3 us (4%)
  between operations  14.6 us (2%)
  local copies, waits for them, and re-layouts  8.06 us (1%)
    convert_element_type x8, other arithmetic, beam_freq(): (real_in * cosine + imag_in * sine).astype(jnp.bfloat16)  190 us
    convert_element_type x8, other arithmetic, beam_freq(): depth_imag = jnp.sin(phase_z).astype(jnp.bfloat16)  98.6 us
    neg x8, other arithmetic, beam_freq(): upper_rows = jnp.concatenate([depth_real, -depth_imag], axis=1)  92.1 us
    psum x1, waiting for transfers between devices, per_device(): summed = lax.psum(local_power, 'sta')  78.1 us
    ppermute x8, waiting for transfers between devices, with_halo(): after = lax.ppermute(leading, axis, down)  37.6 us
    all_gather x1, blocking collectives, per_device(): lax.all_gather(slowness, 'sta', axis=2, tiled=True)[0]  29.4 us
    all_gather x1, waiting for transfers between devices, per_device(): lax.all_gather(aligned, 'sta', axis=2, tiled=True)  21.8 us
    ppermute x8, starting transfers between devices, with_halo(): before = lax.ppermute(last, axis, up)  21.7 us
  transfers between devices with their start and end apart: 18, of which 10 were waited for; matrix products, arithmetic and copies ran while one was open for 0% of the time, Pallas kernels for 0%

commit v1 on v0

--- a/solution.py
+++ b/solution.py
@@ -16,6 +16,11 @@
 CZ = 128
 TWO_PI = 2.0 * math.pi
 BACKGROUND = 0.05
+
+
+def summed_here(value, name):
+    blocks = lax.all_gather(value, name)
+    return jnp.sum(blocks, axis=0)
 
 
 def with_halo(array, sides, width):
@@ -101,7 +106,7 @@
     beams = freq_beams(own_ids, rows, lax.all_gather(slowness, "sta", axis=2, tiled=True)[0])
     squares = jnp.sum(beams * beams, axis=0)
     local_power = squares[:, :CZ] + squares[:, CZ:]
-    summed = lax.psum(local_power, "sta")
+    summed = summed_here(local_power, "sta")
     stacked = (summed / (FREQS * STATIONS) + BACKGROUND).reshape(CX, CY, CZ)
     square_y = band_matrix(spread_taps[1], CY)[:, HALF : HALF + CY]
     square_z = band_matrix(spread_taps[2], CZ)[:, HALF : HALF + CZ]

time: 649 us -> 611 us (0.941)
  waiting for transfers between devices: 138 us -> 106 us
    psum x1 -> x0, waiting for transfers between devices: 78.1 us -> none  [per_device(): summed = lax.psum(local_power, 'sta')]
    all_gather x0 -> x1, waiting for transfers between devices: none -> 45.8 us  [summed_here(): blocks = lax.all_gather(value, name)]
where the time goes in v1:
time: 611 us; the launch traced here: 610 us
  other arithmetic  389 us (64%)
  waiting for transfers between devices  106 us (17%)
  starting transfers between devices  36.1 us (6%)
  blocking collectives  29.4 us (5%)
  matrix products  21.5 us (4%)
  between operations  14.6 us (2%)
  local copies, waits for them, and re-layouts  7.27 us (1%)
    convert_element_type x8, other arithmetic, beam_freq(): (real_in * cosine + imag_in * sine).astype(jnp.bfloat16)  190 us
    convert_element_type x8, other arithmetic, beam_freq(): depth_imag = jnp.sin(phase_z).astype(jnp.bfloat16)  98.6 us
    neg x8, other arithmetic, beam_freq(): upper_rows = jnp.concatenate([depth_real, -depth_imag], axis=1)  92.1 us
    all_gather x1, waiting for transfers between devices, summed_here(): blocks = lax.all_gather(value, name)  45.8 us
    ppermute x8, waiting for transfers between devices, with_halo(): after = lax.ppermute(leading, axis, down)  37.6 us
    all_gather x1, blocking collectives, per_device(): lax.all_gather(slowness, 'sta', axis=2, tiled=True)[0]  29.4 us
    all_gather x1, waiting for transfers between devices, per_device(): lax.all_gather(aligned, 'sta', axis=2, tiled=True)  22.8 us
    ppermute x8, starting transfers between devices, with_halo(): after = lax.ppermute(leading, axis, down)  18.9 us
  transfers between devices with their start and end apart: 18, of which 10 were waited for; matrix products, arithmetic and copies ran while one was open for 0% of the time, Pallas kernels for 0%

profile of v1, /device:TPU:25, one launch (start us, length us, event | category | flops | bytes accessed | tf_op | source)
XLA Modules:
  0.0 610.3 jit_solution(16295328702318096562)
XLA Ops:
  11.0 29.4 %all_gather.13 = bf16[1,3,6144]{2,1,0:T(4,128)(2,1)S(1)} all-gather(bf16[1,3,768]{2,1,0:T(4,128)(2,1)} %param.8), channel_id=1, replica_groups=mesh['grid'=16,'sta'=8] {'sta'}, dimensions={2}, use_global_device_ids=true | all-gather | bytes 41472 | tf_op jit(solution)/shard_map/all_gather | solution.py:106
  40.5 22.8 %all-gather.4.cloned.1.call-done = bf16[64,2,6144]{2,0,1:T(8,128)(2,1)} async-done(((bf16[64,2,768]{2,0,1:T(8,128)(2,1)}), bf16[64,2,6144]{2,0,1:T(8,128)(2,1)}) %all-gather.4.cloned.1.call-update) | async-done | bytes 1572880 | tf_op jit(solution)/shard_map/all_gather | solution.py:104
  64.4 408.7 %while.12 = (s32[]{:T(128)}, f32[8,256,256]{2,1,0:T(8,128)S(1)}, bf16[8,2,6144]{2,1,0:T(2,128)(2,1)S(1)}, s32[8]{0:T(128)S(1)}, bf16[3,6144]{1,0:T(4,128)(2,1)S(...) while((s32[]{:T(128)}, f32[8,256,256]{2,1,0:T(8,128)S(1)}, ...), condition=%wide.region_1.2_spmd, body=%wide.region_0.1_spmd.sunk | while | flops 1669103744 | bytes 24729580 | solution.py:78
  66.0 23.7 %fusion.136 = (bf16[256,6144]{1,0:T(8,128)(2,1)S(1)}, bf16[256,6144]{1,0:T(8,128)(2,1)S(1)}) fusion(f32[6144]{0:T(1024)S(1)} %bitcast.161, f32[8,6144]{1,0:T(8,128)S(1)} %broadcast_multiply_fusion.4, f32[32,6144]{1,0:T(8,128)S(1)} %broadcast_multiply_fusion.5, f32[6144]{0:T(1024)S(1)} %bitcast.160), kind=kLoop, calls=%fused_computation.6.clone.1 | loop fusion | flops 14155776 | bytes 7323648 | tf_op jit(solution)/shard_map/while/body/eval_jaxpr/convert_element_type | solution.py:65
  89.8 12.3 %fusion.134 = (bf16[6144,128]{1,0:T(8,128)(2,1)S(1)}, bf16[6144,128]{1,0:T(8,128)(2,1)S(1)}) fusion(f32[128]{0:T(128)S(1)} %iota_add_fusion.8, f32[6144]{0:T(1024)S(1)} %bitcast.158), kind=kLoop, calls=%fused_computation.26.clone.2 | loop fusion | flops 2359296 | bytes 3170816 | tf_op jit(solution)/shard_map/while/body/eval_jaxpr/convert_element_type | solution.py:70
  102.1 11.5 %fusion.135 = bf16[6144,128]{1,0:T(8,128)(2,1)S(1)} fusion(f32[128]{0:T(128)S(1)} %iota_add_fusion.8, f32[6144]{0:T(1024)S(1)} %bitcast.159), kind=kLoop, calls=%fused_computation.30.clone.1 | loop fusion | flops 3932160 | bytes 1597952 | tf_op jit(solution)/shard_map/while/body/eval_jaxpr/neg | solution.py:71
  117.1 23.7 %fusion.136 = (bf16[256,6144]{1,0:T(8,128)(2,1)S(1)}, bf16[256,6144]{1,0:T(8,128)(2,1)S(1)}) fusion(f32[6144]{0:T(1024)S(1)} %bitcast.161, f32[8,6144]{1,0:T(8,128)S(1)} %broadcast_multiply_fusion.4, f32[32,6144]{1,0:T(8,128)S(1)} %broadcast_multiply_fusion.5, f32[6144]{0:T(1024)S(1)} %bitcast.160), kind=kLoop, calls=%fused_computation.6.clone.1 | loop fusion | flops 14155776 | bytes 7323648 | tf_op jit(solution)/shard_map/while/body/eval_jaxpr/convert_element_type | solution.py:65
  140.9 12.3 %fusion.134 = (bf16[6144,128]{1,0:T(8,128)(2,1)S(1)}, bf16[6144,128]{1,0:T(8,128)(2,1)S(1)}) fusion(f32[128]{0:T(128)S(1)} %iota_add_fusion.8, f32[6144]{0:T(1024)S(1)} %bitcast.158), kind=kLoop, calls=%fused_computation.26.clone.2 | loop fusion | flops 2359296 | bytes 3170816 | tf_op jit(solution)/shard_map/while/body/eval_jaxpr/convert_element_type | solution.py:70
  153.2 11.5 %fusion.135 = bf16[6144,128]{1,0:T(8,128)(2,1)S(1)} fusion(f32[128]{0:T(128)S(1)} %iota_add_fusion.8, f32[6144]{0:T(1024)S(1)} %bitcast.159), kind=kLoop, calls=%fused_computation.30.clone.1 | loop fusion | flops 3932160 | bytes 1597952 | tf_op jit(solution)/shard_map/while/body/eval_jaxpr/neg | solution.py:71
  168.2 23.7 %fusion.136 = (bf16[256,6144]{1,0:T(8,128)(2,1)S(1)}, bf16[256,6144]{1,0:T(8,128)(2,1)S(1)}) fusion(f32[6144]{0:T(1024)S(1)} %bitcast.161, f32[8,6144]{1,0:T(8,128)S(1)} %broadcast_multiply_fusion.4, f32[32,6144]{1,0:T(8,128)S(1)} %broadcast_multiply_fusion.5, f32[6144]{0:T(1024)S(1)} %bitcast.160), kind=kLoop, calls=%fused_computation.6.clone.1 | loop fusion | flops 14155776 | bytes 7323648 | tf_op jit(solution)/shard_map/while/body/eval_jaxpr/convert_element_type | solution.py:65
  192.0 12.3 %fusion.134 = (bf16[6144,128]{1,0:T(8,128)(2,1)S(1)}, bf16[6144,128]{1,0:T(8,128)(2,1)S(1)}) fusion(f32[128]{0:T(128)S(1)} %iota_add_fusion.8, f32[6144]{0:T(1024)S(1)} %bitcast.158), kind=kLoop, calls=%fused_computation.26.clone.2 | loop fusion | flops 2359296 | bytes 3170816 | tf_op jit(solution)/shard_map/while/body/eval_jaxpr/convert_element_type | solution.py:70
  204.3 11.5 %fusion.135 = bf16[6144,128]{1,0:T(8,128)(2,1)S(1)} fusion(f32[128]{0:T(128)S(1)} %iota_add_fusion.8, f32[6144]{0:T(1024)S(1)} %bitcast.159), kind=kLoop, calls=%fused_computation.30.clone.1 | loop fusion | flops 3932160 | bytes 1597952 | tf_op jit(solution)/shard_map/while/body/eval_jaxpr/neg | solution.py:71
  219.3 23.7 %fusion.136 = (bf16[256,6144]{1,0:T(8,128)(2,1)S(1)}, bf16[256,6144]{1,0:T(8,128)(2,1)S(1)}) fusion(f32[6144]{0:T(1024)S(1)} %bitcast.161, f32[8,6144]{1,0:T(8,128)S(1)} %broadcast_multiply_fusion.4, f32[32,6144]{1,0:T(8,128)S(1)} %broadcast_multiply_fusion.5, f32[6144]{0:T(1024)S(1)} %bitcast.160), kind=kLoop, calls=%fused_computation.6.clone.1 | loop fusion | flops 14155776 | bytes 7323648 | tf_op jit(solution)/shard_map/while/body/eval_jaxpr/convert_element_type | solution.py:65
  243.1 12.3 %fusion.134 = (bf16[6144,128]{1,0:T(8,128)(2,1)S(1)}, bf16[6144,128]{1,0:T(8,128)(2,1)S(1)}) fusion(f32[128]{0:T(128)S(1)} %iota_add_fusion.8, f32[6144]{0:T(1024)S(1)} %bitcast.158), kind=kLoop, calls=%fused_computation.26.clone.2 | loop fusion | flops 2359296 | bytes 3170816 | tf_op jit(solution)/shard_map/while/body/eval_jaxpr/convert_element_type | solution.py:70
  255.4 11.5 %fusion.135 = bf16[6144,128]{1,0:T(8,128)(2,1)S(1)} fusion(f32[128]{0:T(128)S(1)} %iota_add_fusion.8, f32[6144]{0:T(1024)S(1)} %bitcast.159), kind=kLoop, calls=%fused_computation.30.clone.1 | loop fusion | flops 3932160 | bytes 1597952 | tf_op jit(solution)/shard_map/while/body/eval_jaxpr/neg | solution.py:71
  270.4 23.7 %fusion.136 = (bf16[256,6144]{1,0:T(8,128)(2,1)S(1)}, bf16[256,6144]{1,0:T(8,128)(2,1)S(1)}) fusion(f32[6144]{0:T(1024)S(1)} %bitcast.161, f32[8,6144]{1,0:T(8,128)S(1)} %broadcast_multiply_fusion.4, f32[32,6144]{1,0:T(8,128)S(1)} %broadcast_multiply_fusion.5, f32[6144]{0:T(1024)S(1)} %bitcast.160), kind=kLoop, calls=%fused_computation.6.clone.1 | loop fusion | flops 14155776 | bytes 7323648 | tf_op jit(solution)/shard_map/while/body/eval_jaxpr/convert_element_type | solution.py:65
  294.2 12.3 %fusion.134 = (bf16[6144,128]{1,0:T(8,128)(2,1)S(1)}, bf16[6144,128]{1,0:T(8,128)(2,1)S(1)}) fusion(f32[128]{0:T(128)S(1)} %iota_add_fusion.8, f32[6144]{0:T(1024)S(1)} %bitcast.158), kind=kLoop, calls=%fused_computation.26.clone.2 | loop fusion | flops 2359296 | bytes 3170816 | tf_op jit(solution)/shard_map/while/body/eval_jaxpr/convert_element_type | solution.py:70
  306.5 11.5 %fusion.135 = bf16[6144,128]{1,0:T(8,128)(2,1)S(1)} fusion(f32[128]{0:T(128)S(1)} %iota_add_fusion.8, f32[6144]{0:T(1024)S(1)} %bitcast.159), kind=kLoop, calls=%fused_computation.30.clone.1 | loop fusion | flops 3932160 | bytes 1597952 | tf_op jit(solution)/shard_map/while/body/eval_jaxpr/neg | solution.py:71
  321.5 23.7 %fusion.136 = (bf16[256,6144]{1,0:T(8,128)(2,1)S(1)}, bf16[256,6144]{1,0:T(8,128)(2,1)S(1)}) fusion(f32[6144]{0:T(1024)S(1)} %bitcast.161, f32[8,6144]{1,0:T(8,128)S(1)} %broadcast_multiply_fusion.4, f32[32,6144]{1,0:T(8,128)S(1)} %broadcast_multiply_fusion.5, f32[6144]{0:T(1024)S(1)} %bitcast.160), kind=kLoop, calls=%fused_computation.6.clone.1 | loop fusion | flops 14155776 | bytes 7323648 | tf_op jit(solution)/shard_map/while/body/eval_jaxpr/convert_element_type | solution.py:65
  345.2 12.3 %fusion.134 = (bf16[6144,128]{1,0:T(8,128)(2,1)S(1)}, bf16[6144,128]{1,0:T(8,128)(2,1)S(1)}) fusion(f32[128]{0:T(128)S(1)} %iota_add_fusion.8, f32[6144]{0:T(1024)S(1)} %bitcast.158), kind=kLoop, calls=%fused_computation.26.clone.2 | loop fusion | flops 2359296 | bytes 3170816 | tf_op jit(solution)/shard_map/while/body/eval_jaxpr/convert_element_type | solution.py:70
  357.6 11.5 %fusion.135 = bf16[6144,128]{1,0:T(8,128)(2,1)S(1)} fusion(f32[128]{0:T(128)S(1)} %iota_add_fusion.8, f32[6144]{0:T(1024)S(1)} %bitcast.159), kind=kLoop, calls=%fused_computation.30.clone.1 | loop fusion | flops 3932160 | bytes 1597952 | tf_op jit(solution)/shard_map/while/body/eval_jaxpr/neg | solution.py:71
  372.6 23.7 %fusion.136 = (bf16[256,6144]{1,0:T(8,128)(2,1)S(1)}, bf16[256,6144]{1,0:T(8,128)(2,1)S(1)}) fusion(f32[6144]{0:T(1024)S(1)} %bitcast.161, f32[8,6144]{1,0:T(8,128)S(1)} %broadcast_multiply_fusion.4, f32[32,6144]{1,0:T(8,128)S(1)} %broadcast_multiply_fusion.5, f32[6144]{0:T(1024)S(1)} %bitcast.160), kind=kLoop, calls=%fused_computation.6.clone.1 | loop fusion | flops 14155776 | bytes 7323648 | tf_op jit(solution)/shard_map/while/body/eval_jaxpr/convert_element_type | solution.py:65
  396.3 12.3 %fusion.134 = (bf16[6144,128]{1,0:T(8,128)(2,1)S(1)}, bf16[6144,128]{1,0:T(8,128)(2,1)S(1)}) fusion(f32[128]{0:T(128)S(1)} %iota_add_fusion.8, f32[6144]{0:T(1024)S(1)} %bitcast.158), kind=kLoop, calls=%fused_computation.26.clone.2 | loop fusion | flops 2359296 | bytes 3170816 | tf_op jit(solution)/shard_map/while/body/eval_jaxpr/convert_element_type | solution.py:70
  408.7 11.5 %fusion.135 = bf16[6144,128]{1,0:T(8,128)(2,1)S(1)} fusion(f32[128]{0:T(128)S(1)} %iota_add_fusion.8, f32[6144]{0:T(1024)S(1)} %bitcast.159), kind=kLoop, calls=%fused_computation.30.clone.1 | loop fusion | flops 3932160 | bytes 1597952 | tf_op jit(solution)/shard_map/while/body/eval_jaxpr/neg | solution.py:71
  423.6 23.7 %fusion.136 = (bf16[256,6144]{1,0:T(8,128)(2,1)S(1)}, bf16[256,6144]{1,0:T(8,128)(2,1)S(1)}) fusion(f32[6144]{0:T(1024)S(1)} %bitcast.161, f32[8,6144]{1,0:T(8,128)S(1)} %broadcast_multiply_fusion.4, f32[32,6144]{1,0:T(8,128)S(1)} %broadcast_multiply_fusion.5, f32[6144]{0:T(1024)S(1)} %bitcast.160), kind=kLoop, calls=%fused_computation.6.clone.1 | loop fusion | flops 14155776 | bytes 7323648 | tf_op jit(solution)/shard_map/while/body/eval_jaxpr/convert_element_type | solution.py:65
  447.4 12.3 %fusion.134 = (bf16[6144,128]{1,0:T(8,128)(2,1)S(1)}, bf16[6144,128]{1,0:T(8,128)(2,1)S(1)}) fusion(f32[128]{0:T(128)S(1)} %iota_add_fusion.8, f32[6144]{0:T(1024)S(1)} %bitcast.158), kind=kLoop, calls=%fused_computation.26.clone.2 | loop fusion | flops 2359296 | bytes 3170816 | tf_op jit(solution)/shard_map/while/body/eval_jaxpr/convert_element_type | solution.py:70
  459.7 11.5 %fusion.135 = bf16[6144,128]{1,0:T(8,128)(2,1)S(1)} fusion(f32[128]{0:T(128)S(1)} %iota_add_fusion.8, f32[6144]{0:T(1024)S(1)} %bitcast.159), kind=kLoop, calls=%fused_computation.30.clone.1 | loop fusion | flops 3932160 | bytes 1597952 | tf_op jit(solution)/shard_map/while/body/eval_jaxpr/neg | solution.py:71
  474.3 45.8 %all-gather.6.cloned.1.call-done = f32[2048,128]{1,0:T(8,128)} async-done(((f32[256,128]{1,0:T(8,128)}), f32[2048,128]{1,0:T(8,128)}) %all-gather.6.cloned.1.call-update) | async-done | bytes 1048592 | tf_op jit(solution)/shard_map/all_gather | solution.py:22
  527.2 5.1 collective-permute-done.1
  537.5 4.8 collective-permute-done.3
  557.4 4.8 collective-permute-done.7
  577.3 4.8 collective-permute-done.11
  (175 shorter events, 91.6 us)
Async XLA Ops:
  7.2 56.1 %all-gather.4.cloned.1.call-start = ((), (), s32[]{:S(2)}) async-start(), calls=%async_computation | async-start | bytes 1769472 | tf_op jit(solution)/shard_map/all_gather | solution.py:104
  11.0 509.2 %all-gather.6.cloned.1.call-start = ((), (), s32[]{:S(2)}) async-start(), calls=%async_computation.1 | async-start | bytes 1179648 | tf_op jit(solution)/shard_map/all_gather | solution.py:22
  64.4 409.6 %copy-start = (f32[3,17]{1,0:T(4,128)S(1)}, f32[3,17]{1,0:T(4,128)}, u32[]{:S(2)}) copy-start(f32[3,17]{1,0:T(4,128)} %param.9) | copy-start | bytes 616
  521.5 5.7 collective-permute-start
  525.2 7.2 %collective-permute-start.1 = (bf16[8,8,128]{2,0,1:T(8,128)(2,1)S(1)}, bf16[8,8,128]{2,0,1:T(8,128)(2,1)S(1)}, u32[]{:S(2)}, u32[]{:S(2)}) collective-permute-start(bf16[8,8,128]{2,0,1:T(8,128)(2,1)S(1)} %get-tuple-element.120), channel_id=1, source_target_pairs={{8,0},{16,8},{24,16},{32,24},{40,32},{48,40},{56,48},{64,56},{72,6... | collective-permute-start | bytes 49160 | tf_op jit(solution)/shard_map/ppermute | solution.py:34
  533.2 4.3 collective-permute-start.2
  535.1 7.2 %collective-permute-start.3 = (bf16[8,8,128]{2,1,0:T(8,128)(2,1)S(1)}, bf16[8,8,128]{2,1,0:T(8,128)(2,1)S(1)}, u32[]{:S(2)}, u32[]{:S(2)}) collective-permute-start(bf16[8,8,128]{2,1,0:T(8,128)(2,1)S(1)} %get-tuple-element.118), channel_id=1, source_target_pairs={{8,0},{16,8},{24,16},{32,24},{40,32},{48,40},{56,48},{64,56},{72,6... | collective-permute-start | bytes 49160 | tf_op jit(solution)/shard_map/ppermute | solution.py:34
  543.1 4.3 collective-permute-start.4
  545.1 7.2 %collective-permute-start.5 = (bf16[8,8,128]{2,1,0:T(8,128)(2,1)S(1)}, bf16[8,8,128]{2,1,0:T(8,128)(2,1)S(1)}, u32[]{:S(2)}, u32[]{:S(2)}) collective-permute-start(bf16[8,8,128]{2,1,0:T(8,128)(2,1)S(1)} %get-tuple-element.116), channel_id=1, source_target_pairs={{8,0},{16,8},{24,16},{32,24},{40,32},{48,40},{56,48},{64,56},{72,6... | collective-permute-start | bytes 49160 | tf_op jit(solution)/shard_map/ppermute | solution.py:34
  553.1 4.3 collective-permute-start.6
  555.0 7.2 %collective-permute-start.7 = (bf16[8,8,128]{2,1,0:T(8,128)(2,1)S(1)}, bf16[8,8,128]{2,1,0:T(8,128)(2,1)S(1)}, u32[]{:S(2)}, u32[]{:S(2)}) collective-permute-start(bf16[8,8,128]{2,1,0:T(8,128)(2,1)S(1)} %get-tuple-element.114), channel_id=1, source_target_pairs={{8,0},{16,8},{24,16},{32,24},{40,32},{48,40},{56,48},{64,56},{72,6... | collective-permute-start | bytes 49160 | tf_op jit(solution)/shard_map/ppermute | solution.py:34
  563.0 4.5 collective-permute-start.8
  565.0 7.2 %collective-permute-start.9 = (bf16[8,8,128]{2,1,0:T(8,128)(2,1)S(1)}, bf16[8,8,128]{2,1,0:T(8,128)(2,1)S(1)}, u32[]{:S(2)}, u32[]{:S(2)}) collective-permute-start(bf16[8,8,128]{2,1,0:T(8,128)(2,1)S(1)} %get-tuple-element.112), channel_id=1, source_target_pairs={{8,0},{16,8},{24,16},{32,24},{40,32},{48,40},{56,48},{64,56},{72,6... | collective-permute-start | bytes 49160 | tf_op jit(solution)/shard_map/ppermute | solution.py:34
  573.0 4.3 collective-permute-start.10
  574.9 7.2 %collective-permute-start.11 = (bf16[8,8,128]{2,1,0:T(8,128)(2,1)S(1)}, bf16[8,8,128]{2,1,0:T(8,128)(2,1)S(1)}, u32[]{:S(2)}, u32[]{:S(2)}) collective-permute-start(bf16[8,8,128]{2,1,0:T(8,128)(2,1)S(1)} %get-tuple-element.110), channel_id=1, source_target_pairs={{8,0},{16,8},{24,16},{32,24},{40,32},{48,40},{56,48},{64,56},{72,6... | collective-permute-start | bytes 49160 | tf_op jit(solution)/shard_map/ppermute | solution.py:34
  582.9 4.3 collective-permute-start.12
  584.9 7.2 %collective-permute-start.13 = (bf16[8,8,128]{2,1,0:T(8,128)(2,1)S(1)}, bf16[8,8,128]{2,1,0:T(8,128)(2,1)S(1)}, u32[]{:S(2)}, u32[]{:S(2)}) collective-permute-start(bf16[8,8,128]{2,1,0:T(8,128)(2,1)S(1)} %get-tuple-element.108), channel_id=1, source_target_pairs={{8,0},{16,8},{24,16},{32,24},{40,32},{48,40},{56,48},{64,56},{72,6... | collective-permute-start | bytes 49160 | tf_op jit(solution)/shard_map/ppermute | solution.py:34
  592.9 5.0 collective-permute-start.14
  594.8 7.2 %collective-permute-start.15 = (bf16[8,8,128]{2,1,0:T(8,128)(2,1)S(1)}, bf16[8,8,128]{2,1,0:T(8,128)(2,1)S(1)}, u32[]{:S(2)}, u32[]{:S(2)}) collective-permute-start(bf16[8,8,128]{2,1,0:T(8,128)(2,1)S(1)} %get-tuple-element.106), channel_id=1, source_target_pairs={{8,0},{16,8},{24,16},{32,24},{40,32},{48,40},{56,48},{64,56},{72,6... | collective-permute-start | bytes 49160 | tf_op jit(solution)/shard_map/ppermute | solution.py:34
Sparse Core Ops, SparseCore 0:
  11.1 52.1 all-gather.3
  474.1 46.0 all-gather.5
